TPU v7x, 32 devices: a whole 2x2x4 slice. The times are simulated.
32 devices in a mesh: sec: 4 (over x, core), row: 4 (over z), col: 2 (over y).
Axes of the slice: x: 2, y: 2, z: 4, core: 2. Of those that a mesh axis runs over, the one named last changes fastest.
Arguments:
- forcing: float32 [4, 8192, 128], P('sec', ('row', 'col')), may hold values from -6 to 6
- inverse_factor: bfloat16 [4, 2, 8192, 8192], P('sec', None, 'col', 'row'), as said below
- diag_inverse: float32 [4, 2, 8192], P('sec', None, 'col'), may hold values from -0.6 to 0.6
- coupling: float32 [4, 2, 8192], P('sec', None, ('row', 'col')), may hold values from -0.8 to 0.8
Outputs:
- section_fields: float32 [4, 8192, 128], P('sec', ('row', 'col'))
Inputs may be any that keep to these rules, and one draw needn't show every extreme that they name: `inverse_factor`: each section's factor is lower triangular: entries above the diagonal are zero in both parts.
All inputs are finite; a program needn't handle non-finite values.
Results may differ from a plain program's by a relative error of at most 0.03.
Values may be sent and summed in bfloat16 or wider, within the bound.
A program may use at most 128 MiB of HBM per device.

v0:
```python
import jax
import jax.numpy as jnp
from jax import lax
from jax.sharding import PartitionSpec as P


def shifted(value, axis, steps):
    count = lax.axis_size(axis)
    initial, last = (max(0, -steps), min(count, count - steps))
    return lax.ppermute(value, axis, [(source, source + steps) for source in range(initial, last)])


def complex_rows(coef_re, coef_im, values, half):
    v_re = values[:, :half]
    v_im = values[:, half:]
    out_re = coef_re[:, None] * v_re - coef_im[:, None] * v_im
    out_im = coef_re[:, None] * v_im + coef_im[:, None] * v_re
    return jnp.concatenate([out_re, out_im], axis=1)


def combine_stack(product):
    half = product.shape[2] // 2
    out_re = product[0, :, :half] - product[1, :, half:]
    out_im = product[0, :, half:] + product[1, :, :half]
    return jnp.concatenate([out_re, out_im], axis=1)


def solve_section(source, factor, dinv):
    width = source.shape[1]
    product = jnp.einsum(
        "kij,jb->kib",
        factor,
        lax.all_gather(source, "col", axis=0, tiled=True),
        preferred_element_type=jnp.float32,
    )
    forward = combine_stack(product)
    share = lax.psum_scatter(
        forward.astype(jnp.bfloat16), "row", scatter_dimension=0, tiled=True
    ).astype(jnp.float32)
    share_rows = share.shape[0]
    local_dinv = lax.dynamic_slice_in_dim(dinv, lax.axis_index("row") * share_rows, share_rows, 1)
    scaled = complex_rows(local_dinv[0], local_dinv[1], share, width // 2).astype(jnp.bfloat16)
    product = jnp.einsum(
        "kij,ib->kjb",
        factor,
        lax.all_gather(scaled, "row", axis=0, tiled=True),
        preferred_element_type=jnp.float32,
    )
    back = combine_stack(product)
    return lax.psum_scatter(
        back.astype(jnp.bfloat16), "col", scatter_dimension=0, tiled=True
    ).astype(jnp.float32)


def local(forcing, inverse_factor, diag_inverse, coupling):
    sections = lax.axis_size("sec")
    section_id = lax.axis_index("sec")
    local_rhs = forcing[0]
    factor = inverse_factor[0]
    dinv = diag_inverse[0]
    couple = coupling[0]
    rows_here = local_rhs.shape[0]
    half = local_rhs.shape[1] // 2
    block_count = 1
    block_width = half // block_count
    rhs_blocks = local_rhs.reshape(rows_here, 2, block_count, block_width)
    results = jnp.zeros((rows_here, 2, block_count, block_width), jnp.float32)
    outgoing = jnp.zeros((rows_here, 2 * block_width), jnp.float32)
    for step_index in range(block_count + sections - 1):
        if step_index > 0:
            incoming = shifted(outgoing.astype(jnp.bfloat16), "sec", 1).astype(outgoing.dtype)
        else:
            incoming = jnp.zeros((rows_here, 2 * block_width), jnp.float32)
        block_index = step_index - section_id
        active = jnp.logical_and(block_index >= 0, block_index < block_count)
        safe_index = jnp.clip(block_index, 0, block_count - 1)
        current = lax.dynamic_index_in_dim(rhs_blocks, safe_index, 2, keepdims=False)
        current = current.reshape(rows_here, 2 * block_width)
        source = (current - complex_rows(couple[0], couple[1], incoming, block_width)).astype(
            jnp.bfloat16
        )
        field = solve_section(source, factor, dinv)
        updated = lax.dynamic_update_index_in_dim(
            results, field.reshape(rows_here, 2, block_width), safe_index, 2
        )
        results = jnp.where(active, updated, results)
        outgoing = field
    return results.reshape(1, rows_here, 2 * half)


def solution(mesh):
    placed = (
        P("sec", ("row", "col"), None),
        P("sec", None, "col", "row"),
        P("sec", None, "col"),
        P("sec", None, ("row", "col")),
    )
    return jax.shard_map(
        local, mesh=mesh, in_specs=placed, out_specs=P("sec", ("row", "col"), None), check_vma=False
    )
```

profile of v0, /device:TPU:0, one launch (start us, length us, event | category | flops | bytes accessed | tf_op | source)
XLA Modules:
  0.0 482.2 jit_solution(10238314074252563666)
XLA Ops:
  7.3 1.2 copy.5
  8.7 9.9 %all_gather.24 = bf16[2048,128]{0,1:T(8,128)(2,1)S(1)} all-gather(bf16[1024,128]{0,1:T(8,128)(2,1)S(1)} %fusion.68), channel_id=1, replica_groups=mesh['sec'=4,'row'=4,'col'=2] {'col'}, dimensions={0}, use_global_device_ids=true | all-gather | bytes 786432 | tf_op jit(solution)/shard_map/all_gather | solution.py:33
  18.6 16.3 %fusion.16 = f32[2,4096,128]{1,2,0:T(8,128)S(1)} fusion(bf16[1,2,4096,2048]{3,2,1,0:T(8,128)(2,1)} %param.5, bf16[2048,128]{0,1:T(8,128)(2,1)S(1)} %all_gather.24), kind=kOutput, calls=%fused_computation.16 | convolution fusion | flops 4294967296 | bytes 38273024 | tf_op jit(solution)/shard_map/kij,jb->kib/dot_general | solution.py:30
  37.2 27.9 %reduce-scatter.9.cloned.1.call-done = bf16[1024,128]{0,1:T(8,128)(2,1)} async-done(((bf16[4096,128]{0,1:T(8,128)(2,1)}), bf16[1024,128]{0,1:T(8,128)(2,1)}) %reduce-scatter.9.cloned.1.call-update) | async-done | bytes 262160 | tf_op jit(solution)/shard_map/reduce_scatter | solution.py:37
  66.9 26.7 %all-gather.5.cloned.1.call-done = bf16[4096,128]{0,1:T(8,128)(2,1)} async-done(((bf16[1024,128]{0,1:T(8,128)(2,1)}), bf16[4096,128]{0,1:T(8,128)(2,1)}) %all-gather.5.cloned.1.call-update) | async-done | bytes 1048592 | tf_op jit(solution)/shard_map/all_gather | solution.py:46
  93.6 13.2 %fusion.28 = f32[2,2048,128]{1,2,0:T(8,128)S(1)} fusion(bf16[1,2,4096,2048]{3,2,1,0:T(8,128)(2,1)} %param.5, bf16[4096,128]{0,1:T(8,128)(2,1)} %all-gather.5.cloned.1.call-done), kind=kOutput, calls=%fused_computation.20 | convolution fusion | flops 4294967296 | bytes 36700160 | tf_op jit(solution)/shard_map/kij,ib->kjb/dot_general | solution.py:43
  107.9 14.2 %reduce-scatter.11.cloned.1.call-done = bf16[1024,128]{0,1:T(8,128)(2,1)} async-done(((bf16[2048,128]{0,1:T(8,128)(2,1)}), bf16[1024,128]{0,1:T(8,128)(2,1)}) %reduce-scatter.11.cloned.1.call-update) | async-done | bytes 262160 | tf_op jit(solution)/shard_map/reduce_scatter | solution.py:50
  122.0 1.7 collective-permute-start
  123.8 1.3 collective-permute-done
  125.3 7.0 %all_gather.26 = bf16[2048,128]{0,1:T(8,128)(2,1)S(1)} all-gather(bf16[1024,128]{0,1:T(8,128)(2,1)S(1)} %fusion.69), channel_id=1, replica_groups=mesh['sec'=4,'row'=4,'col'=2] {'col'}, dimensions={0}, use_global_device_ids=true | all-gather | bytes 786432 | tf_op jit(solution)/shard_map/all_gather | solution.py:33
  132.4 16.3 %fusion.19 = f32[2,4096,128]{1,2,0:T(8,128)S(1)} fusion(bf16[1,2,4096,2048]{3,2,1,0:T(8,128)(2,1)} %param.5, bf16[2048,128]{0,1:T(8,128)(2,1)S(1)} %all_gather.26), kind=kOutput, calls=%fused_computation.17 | convolution fusion | flops 4294967296 | bytes 38273024 | tf_op jit(solution)/shard_map/kij,jb->kib/dot_general | solution.py:30
  150.0 32.0 %reduce-scatter.13.cloned.1.call-done = bf16[1024,128]{0,1:T(8,128)(2,1)} async-done(((bf16[4096,128]{0,1:T(8,128)(2,1)}), bf16[1024,128]{0,1:T(8,128)(2,1)}) %reduce-scatter.13.cloned.1.call-update) | async-done | bytes 262160 | tf_op jit(solution)/shard_map/reduce_scatter | solution.py:37
  184.1 26.5 %all-gather.7.cloned.1.call-done = bf16[4096,128]{0,1:T(8,128)(2,1)} async-done(((bf16[1024,128]{0,1:T(8,128)(2,1)}), bf16[4096,128]{0,1:T(8,128)(2,1)}) %all-gather.7.cloned.1.call-update) | async-done | bytes 1048592 | tf_op jit(solution)/shard_map/all_gather | solution.py:46
  210.6 13.2 %fusion.31 = f32[2,2048,128]{1,2,0:T(8,128)S(1)} fusion(bf16[1,2,4096,2048]{3,2,1,0:T(8,128)(2,1)} %param.5, bf16[4096,128]{0,1:T(8,128)(2,1)} %all-gather.7.cloned.1.call-done), kind=kOutput, calls=%fused_computation.21 | convolution fusion | flops 4294967296 | bytes 36700160 | tf_op jit(solution)/shard_map/kij,ib->kjb/dot_general | solution.py:43
  224.9 14.2 %reduce-scatter.15.cloned.1.call-done = bf16[1024,128]{0,1:T(8,128)(2,1)} async-done(((bf16[2048,128]{0,1:T(8,128)(2,1)}), bf16[1024,128]{0,1:T(8,128)(2,1)}) %reduce-scatter.15.cloned.1.call-update) | async-done | bytes 262160 | tf_op jit(solution)/shard_map/reduce_scatter | solution.py:50
  239.0 1.7 collective-permute-start.1
  240.8 1.3 collective-permute-done.1
  242.3 7.0 %all_gather.28 = bf16[2048,128]{0,1:T(8,128)(2,1)S(1)} all-gather(bf16[1024,128]{0,1:T(8,128)(2,1)S(1)} %fusion.70), channel_id=1, replica_groups=mesh['sec'=4,'row'=4,'col'=2] {'col'}, dimensions={0}, use_global_device_ids=true | all-gather | bytes 786432 | tf_op jit(solution)/shard_map/all_gather | solution.py:33
  249.3 16.3 %fusion.22 = f32[2,4096,128]{1,2,0:T(8,128)S(1)} fusion(bf16[1,2,4096,2048]{3,2,1,0:T(8,128)(2,1)} %param.5, bf16[2048,128]{0,1:T(8,128)(2,1)S(1)} %all_gather.28), kind=kOutput, calls=%fused_computation.18 | convolution fusion | flops 4294967296 | bytes 38273024 | tf_op jit(solution)/shard_map/kij,jb->kib/dot_general | solution.py:30
  267.0 32.0 %reduce-scatter.17.cloned.1.call-done = bf16[1024,128]{0,1:T(8,128)(2,1)} async-done(((bf16[4096,128]{0,1:T(8,128)(2,1)}), bf16[1024,128]{0,1:T(8,128)(2,1)}) %reduce-scatter.17.cloned.1.call-update) | async-done | bytes 262160 | tf_op jit(solution)/shard_map/reduce_scatter | solution.py:37
  300.9 26.7 %all-gather.9.cloned.1.call-done = bf16[4096,128]{0,1:T(8,128)(2,1)} async-done(((bf16[1024,128]{0,1:T(8,128)(2,1)}), bf16[4096,128]{0,1:T(8,128)(2,1)}) %all-gather.9.cloned.1.call-update) | async-done | bytes 1048592 | tf_op jit(solution)/shard_map/all_gather | solution.py:46
  327.6 13.2 %fusion.34 = f32[2,2048,128]{1,2,0:T(8,128)S(1)} fusion(bf16[1,2,4096,2048]{3,2,1,0:T(8,128)(2,1)} %param.5, bf16[4096,128]{0,1:T(8,128)(2,1)} %all-gather.9.cloned.1.call-done), kind=kOutput, calls=%fused_computation.22 | convolution fusion | flops 4294967296 | bytes 36700160 | tf_op jit(solution)/shard_map/kij,ib->kjb/dot_general | solution.py:43
  341.8 14.2 %reduce-scatter.19.cloned.1.call-done = bf16[1024,128]{0,1:T(8,128)(2,1)} async-done(((bf16[2048,128]{0,1:T(8,128)(2,1)}), bf16[1024,128]{0,1:T(8,128)(2,1)}) %reduce-scatter.19.cloned.1.call-update) | async-done | bytes 262160 | tf_op jit(solution)/shard_map/reduce_scatter | solution.py:50
  356.0 1.7 collective-permute-start.2
  357.7 1.3 collective-permute-done.2
  359.2 7.3 %all_gather.30 = bf16[2048,128]{0,1:T(8,128)(2,1)S(1)} all-gather(bf16[1024,128]{0,1:T(8,128)(2,1)S(1)} %fusion.71), channel_id=1, replica_groups=mesh['sec'=4,'row'=4,'col'=2] {'col'}, dimensions={0}, use_global_device_ids=true | all-gather | bytes 786432 | tf_op jit(solution)/shard_map/all_gather | solution.py:33
  366.5 16.3 %fusion.25 = f32[2,4096,128]{1,2,0:T(8,128)S(1)} fusion(bf16[1,2,4096,2048]{3,2,1,0:T(8,128)(2,1)} %param.5, bf16[2048,128]{0,1:T(8,128)(2,1)S(1)} %all_gather.30), kind=kOutput, calls=%fused_computation.19 | convolution fusion | flops 4294967296 | bytes 38273024 | tf_op jit(solution)/shard_map/kij,jb->kib/dot_general | solution.py:30
  384.2 32.0 %reduce-scatter.21.cloned.1.call-done = bf16[1024,128]{0,1:T(8,128)(2,1)} async-done(((bf16[4096,128]{0,1:T(8,128)(2,1)}), bf16[1024,128]{0,1:T(8,128)(2,1)}) %reduce-scatter.21.cloned.1.call-update) | async-done | bytes 262160 | tf_op jit(solution)/shard_map/reduce_scatter | solution.py:37
  418.1 26.7 %all-gather.11.cloned.1.call-done = bf16[4096,128]{0,1:T(8,128)(2,1)} async-done(((bf16[1024,128]{0,1:T(8,128)(2,1)}), bf16[4096,128]{0,1:T(8,128)(2,1)}) %all-gather.11.cloned.1.call-update) | async-done | bytes 1048592 | tf_op jit(solution)/shard_map/all_gather | solution.py:46
  444.8 13.2 %fusion.37 = f32[2,2048,128]{1,2,0:T(8,128)S(1)} fusion(bf16[1,2,4096,2048]{3,2,1,0:T(8,128)(2,1)} %param.5, bf16[4096,128]{0,1:T(8,128)(2,1)} %all-gather.11.cloned.1.call-done), kind=kOutput, calls=%fused_computation.23 | convolution fusion | flops 4294967296 | bytes 36700160 | tf_op jit(solution)/shard_map/kij,ib->kjb/dot_general | solution.py:43
  459.0 14.2 %reduce-scatter.23.cloned.1.call-done = bf16[1024,128]{0,1:T(8,128)(2,1)} async-done(((bf16[2048,128]{0,1:T(8,128)(2,1)}), bf16[1024,128]{0,1:T(8,128)(2,1)}) %reduce-scatter.23.cloned.1.call-update) | async-done | bytes 262160 | tf_op jit(solution)/shard_map/reduce_scatter | solution.py:50
  473.2 1.1 select_bitcast_fusion
  (74 shorter events, 20.0 us)
Async XLA Ops:
  6.5 58.5 %reduce-scatter.9.cloned.1.call-start = ((), (), s32[]{:S(2)}) async-start(), calls=%async_computation.8 | async-start | bytes 1310720 | tf_op jit(solution)/shard_map/reduce_scatter | solution.py:37
  36.3 57.4 %all-gather.5.cloned.1.call-start = ((), (), s32[]{:S(2)}) async-start(), calls=%async_computation.9 | async-start | bytes 1310720 | tf_op jit(solution)/shard_map/all_gather | solution.py:46
  66.9 55.1 %reduce-scatter.11.cloned.1.call-start = ((), (), s32[]{:S(2)}) async-start(), calls=%async_computation.10 | async-start | bytes 786432 | tf_op jit(solution)/shard_map/reduce_scatter | solution.py:50
  107.8 74.2 %reduce-scatter.13.cloned.1.call-start = ((), (), s32[]{:S(2)}) async-start(), calls=%async_computation.11 | async-start | bytes 1310720 | tf_op jit(solution)/shard_map/reduce_scatter | solution.py:37
  122.0 3.1 collective-permute-start
  150.0 60.7 %all-gather.7.cloned.1.call-start = ((), (), s32[]{:S(2)}) async-start(), calls=%async_computation.12 | async-start | bytes 1310720 | tf_op jit(solution)/shard_map/all_gather | solution.py:46
  183.9 55.1 %reduce-scatter.15.cloned.1.call-start = ((), (), s32[]{:S(2)}) async-start(), calls=%async_computation.13 | async-start | bytes 786432 | tf_op jit(solution)/shard_map/reduce_scatter | solution.py:50
  224.8 74.2 %reduce-scatter.17.cloned.1.call-start = ((), (), s32[]{:S(2)}) async-start(), calls=%async_computation.14 | async-start | bytes 1310720 | tf_op jit(solution)/shard_map/reduce_scatter | solution.py:37
  239.0 3.1 collective-permute-start.1
  266.9 60.6 %all-gather.9.cloned.1.call-start = ((), (), s32[]{:S(2)}) async-start(), calls=%async_computation.15 | async-start | bytes 1310720 | tf_op jit(solution)/shard_map/all_gather | solution.py:46
  300.9 55.1 %reduce-scatter.19.cloned.1.call-start = ((), (), s32[]{:S(2)}) async-start(), calls=%async_computation.16 | async-start | bytes 786432 | tf_op jit(solution)/shard_map/reduce_scatter | solution.py:50
  341.8 74.4 %reduce-scatter.21.cloned.1.call-start = ((), (), s32[]{:S(2)}) async-start(), calls=%async_computation.17 | async-start | bytes 1310720 | tf_op jit(solution)/shard_map/reduce_scatter | solution.py:37
  356.0 3.1 collective-permute-start.2
  384.1 60.6 %all-gather.11.cloned.1.call-start = ((), (), s32[]{:S(2)}) async-start(), calls=%async_computation.18 | async-start | bytes 1310720 | tf_op jit(solution)/shard_map/all_gather | solution.py:46
  418.0 55.2 %reduce-scatter.23.cloned.1.call-start = ((), (), s32[]{:S(2)}) async-start(), calls=%async_computation.19 | async-start | bytes 786432 | tf_op jit(solution)/shard_map/reduce_scatter | solution.py:50
  458.0 15.2 %copy-start = (bf16[1024,128]{0,1:T(8,128)(2,1)S(1)}, bf16[1024,128]{0,1:T(8,128)(2,1)}, u32[]{:S(2)}) copy-start(bf16[1024,128]{0,1:T(8,128)(2,1)} %reduce-scatter.11.cloned.1.call-done) | copy-start | bytes 786436
  458.0 15.2 %copy-start.1 = (bf16[1024,128]{0,1:T(8,128)(2,1)S(1)}, bf16[1024,128]{0,1:T(8,128)(2,1)}, u32[]{:S(2)}) copy-start(bf16[1024,128]{0,1:T(8,128)(2,1)} %reduce-scatter.15.cloned.1.call-done) | copy-start | bytes 786436
  458.0 15.2 %copy-start.2 = (bf16[1024,128]{0,1:T(8,128)(2,1)S(1)}, bf16[1024,128]{0,1:T(8,128)(2,1)}, u32[]{:S(2)}) copy-start(bf16[1024,128]{0,1:T(8,128)(2,1)} %reduce-scatter.19.cloned.1.call-done) | copy-start | bytes 786436
Sparse Core Ops, SparseCore 0:
  36.4 28.6 reduce-scatter.8
  67.0 26.5 all-gather.4
  107.9 14.0 reduce-scatter.10
  150.1 31.9 reduce-scatter.12
  184.0 26.5 all-gather.6
  224.9 14.0 reduce-scatter.14
  267.1 31.9 reduce-scatter.16
  301.0 26.5 all-gather.8
  341.9 14.0 reduce-scatter.18
  384.2 31.9 reduce-scatter.20
  418.1 26.5 all-gather.10
  459.1 14.0 reduce-scatter.22
where the time goes:
time: 483 us; the launch traced here: 482 us
  waiting for transfers between devices  291 us (60%)
  matrix products  118 us (24%)
  blocking collectives  31.3 us (6%)
  other arithmetic  17.6 us (4%)
  between operations  13.9 us (3%)
  starting transfers between devices  5.87 us (1%)
    reduce_scatter x4, waiting for transfers between devices, solve_section(): lax.psum_scatter(forward.astype(jnp.bfloat16), 'row', scatter_dimension=0...  124 us
    all_gather x4, waiting for transfers between devices, solve_section(): lax.all_gather(scaled, 'row', axis=0, tiled=True)  107 us
    dot_general x4, matrix products, solve_section(): jnp.einsum('kij,jb->kib', factor, lax.all_gather(source, 'col', axis=0, t...  65.2 us
    reduce_scatter x4, waiting for transfers between devices, solve_section(): lax.psum_scatter(back.astype(jnp.bfloat16), 'col', scatter_dimension=0, t...  56.6 us
    dot_general x4, matrix products, solve_section(): jnp.einsum('kij,ib->kjb', factor, lax.all_gather(scaled, 'row', axis=0, t...  52.8 us
    all_gather x4, blocking collectives, solve_section(): lax.all_gather(source, 'col', axis=0, tiled=True)  31.3 us
  transfers between devices with their start and end apart: 15, of which 15 were waited for; matrix products, arithmetic and copies ran while one was open for 0% of the time, Pallas kernels for 0%

commit v1 on v0

--- a/solution.py
+++ b/solution.py
@@ -2,6 +2,11 @@
 import jax.numpy as jnp
 from jax import lax
 from jax.sharding import PartitionSpec as P
+
+
+def tiled_gather(array, axis, dim):
+    copies = jnp.concatenate([array] * lax.axis_size(axis), axis=dim)
+    return lax.all_to_all(copies, axis, dim, dim, tiled=True)
 
 
 def shifted(value, axis, steps):
@@ -28,10 +33,7 @@
 def solve_section(source, factor, dinv):
     width = source.shape[1]
     product = jnp.einsum(
-        "kij,jb->kib",
-        factor,
-        lax.all_gather(source, "col", axis=0, tiled=True),
-        preferred_element_type=jnp.float32,
+        "kij,jb->kib", factor, tiled_gather(source, "col", 0), preferred_element_type=jnp.float32
     )
     forward = combine_stack(product)
     share = lax.psum_scatter(

time: 483 us -> 494 us (1.023)
  blocking collectives: 31.3 us -> 39 us
    all_to_all x0 -> x4, blocking collectives: none -> 39 us  [tiled_gather(): return lax.all_to_all(copies, axis, dim, dim, tiled=True)]
    all_gather x4 -> x0, blocking collectives: 31.3 us -> none  [solve_section(): lax.all_gather(source, 'col', axis=0, tiled=True)]
where the time goes in v1:
time: 494 us; the launch traced here: 493 us
  waiting for transfers between devices  290 us (59%)
  matrix products  118 us (24%)
  blocking collectives  39 us (8%)
  other arithmetic  17.8 us (4%)
  between operations  14 us (3%)
  local copies, waits for them, and re-layouts  7.78 us (2%)
  starting transfers between devices  5.91 us (1%)
    reduce_scatter x4, waiting for transfers between devices, solve_section(): lax.psum_scatter(forward.astype(jnp.bfloat16), 'row', scatter_dimension=0...  123 us
    all_gather x4, waiting for transfers between devices, solve_section(): lax.all_gather(scaled, 'row', axis=0, tiled=True)  107 us
    dot_general x4, matrix products, solve_section(): jnp.einsum('kij,jb->kib', factor, tiled_gather(source, 'col', 0), preferr...  65.3 us
    reduce_scatter x4, waiting for transfers between devices, solve_section(): lax.psum_scatter(back.astype(jnp.bfloat16), 'col', scatter_dimension=0, t...  56.6 us
    dot_general x4, matrix products, solve_section(): jnp.einsum('kij,ib->kjb', factor, lax.all_gather(scaled, 'row', axis=0, t...  52.8 us
    all_to_all x4, blocking collectives, tiled_gather(): return lax.all_to_all(copies, axis, dim, dim, tiled=True)  39 us
  transfers between devices with their start and end apart: 15, of which 15 were waited for; matrix products, arithmetic and copies ran while one was open for 0% of the time, Pallas kernels for 0%

profile of v1, /device:TPU:0, one launch (start us, length us, event | category | flops | bytes accessed | tf_op | source)
XLA Modules:
  0.0 493.0 jit_solution(3584544687681358770)
XLA Ops:
  7.3 1.2 copy.7
  8.8 12.0 %all_to_all.48 = bf16[2,1024,128]{1,2,0:T(8,128)(2,1)S(1)} all-to-all(bf16[2,1024,128]{1,2,0:T(8,128)(2,1)S(1)} %bitcast.133), channel_id=1, replica_groups=mesh['sec'=4,'row'=4,'col'=2] {'col'}, dimensions={0} | all-to-all | bytes 1048576 | tf_op jit(solution)/shard_map/all_to_all | solution.py:9
  21.8 16.3 %fusion.16 = f32[2,4096,128]{1,2,0:T(8,128)S(1)} fusion(bf16[2048,128,1]{0,1,2:T(8,128)(2,1)S(1)} %reshape.97, bf16[1,2,4096,2048]{3,2,1,0:T(8,128)(2,1)} %param.5), kind=kOutput, calls=%fused_computation.16 | convolution fusion | flops 4294967296 | bytes 38273024 | tf_op jit(solution)/shard_map/kij,jb->kib/dot_general | solution.py:35
  40.3 26.8 %reduce-scatter.9.cloned.1.call-done = bf16[1024,128]{0,1:T(8,128)(2,1)} async-done(((bf16[4096,128]{0,1:T(8,128)(2,1)}), bf16[1024,128]{0,1:T(8,128)(2,1)}) %reduce-scatter.9.cloned.1.call-update) | async-done | bytes 262160 | tf_op jit(solution)/shard_map/reduce_scatter | solution.py:39
  69.0 26.7 %all-gather.5.cloned.1.call-done = bf16[4096,128]{0,1:T(8,128)(2,1)} async-done(((bf16[1024,128]{0,1:T(8,128)(2,1)}), bf16[4096,128]{0,1:T(8,128)(2,1)}) %all-gather.5.cloned.1.call-update) | async-done | bytes 1048592 | tf_op jit(solution)/shard_map/all_gather | solution.py:48
  95.7 13.2 %fusion.28 = f32[2,2048,128]{1,2,0:T(8,128)S(1)} fusion(bf16[1,2,4096,2048]{3,2,1,0:T(8,128)(2,1)} %param.5, bf16[4096,128]{0,1:T(8,128)(2,1)} %all-gather.5.cloned.1.call-done), kind=kOutput, calls=%fused_computation.20 | convolution fusion | flops 4294967296 | bytes 36700160 | tf_op jit(solution)/shard_map/kij,ib->kjb/dot_general | solution.py:45
  109.9 14.2 %reduce-scatter.11.cloned.1.call-done = bf16[1024,128]{0,1:T(8,128)(2,1)} async-done(((bf16[2048,128]{0,1:T(8,128)(2,1)}), bf16[1024,128]{0,1:T(8,128)(2,1)}) %reduce-scatter.11.cloned.1.call-update) | async-done | bytes 262160 | tf_op jit(solution)/shard_map/reduce_scatter | solution.py:52
  124.1 1.7 collective-permute-start
  125.8 1.3 collective-permute-done
  127.4 9.0 %all_to_all.49 = bf16[2,1024,128]{1,2,0:T(8,128)(2,1)S(1)} all-to-all(bf16[2,1024,128]{1,2,0:T(8,128)(2,1)S(1)} %bitcast.135), channel_id=1, replica_groups=mesh['sec'=4,'row'=4,'col'=2] {'col'}, dimensions={0} | all-to-all | bytes 1048576 | tf_op jit(solution)/shard_map/all_to_all | solution.py:9
  137.4 16.3 %fusion.19 = f32[2,4096,128]{1,2,0:T(8,128)S(1)} fusion(bf16[2048,128,1]{0,1,2:T(8,128)(2,1)S(1)} %reshape.99, bf16[1,2,4096,2048]{3,2,1,0:T(8,128)(2,1)} %param.5), kind=kOutput, calls=%fused_computation.17 | convolution fusion | flops 4294967296 | bytes 38273024 | tf_op jit(solution)/shard_map/kij,jb->kib/dot_general | solution.py:35
  155.0 32.0 %reduce-scatter.13.cloned.1.call-done = bf16[1024,128]{0,1:T(8,128)(2,1)} async-done(((bf16[4096,128]{0,1:T(8,128)(2,1)}), bf16[1024,128]{0,1:T(8,128)(2,1)}) %reduce-scatter.13.cloned.1.call-update) | async-done | bytes 262160 | tf_op jit(solution)/shard_map/reduce_scatter | solution.py:39
  189.0 26.7 %all-gather.7.cloned.1.call-done = bf16[4096,128]{0,1:T(8,128)(2,1)} async-done(((bf16[1024,128]{0,1:T(8,128)(2,1)}), bf16[4096,128]{0,1:T(8,128)(2,1)}) %all-gather.7.cloned.1.call-update) | async-done | bytes 1048592 | tf_op jit(solution)/shard_map/all_gather | solution.py:48
  215.7 13.2 %fusion.31 = f32[2,2048,128]{1,2,0:T(8,128)S(1)} fusion(bf16[1,2,4096,2048]{3,2,1,0:T(8,128)(2,1)} %param.5, bf16[4096,128]{0,1:T(8,128)(2,1)} %all-gather.7.cloned.1.call-done), kind=kOutput, calls=%fused_computation.21 | convolution fusion | flops 4294967296 | bytes 36700160 | tf_op jit(solution)/shard_map/kij,ib->kjb/dot_general | solution.py:45
  229.9 14.2 %reduce-scatter.15.cloned.1.call-done = bf16[1024,128]{0,1:T(8,128)(2,1)} async-done(((bf16[2048,128]{0,1:T(8,128)(2,1)}), bf16[1024,128]{0,1:T(8,128)(2,1)}) %reduce-scatter.15.cloned.1.call-update) | async-done | bytes 262160 | tf_op jit(solution)/shard_map/reduce_scatter | solution.py:52
  244.0 1.7 collective-permute-start.1
  245.8 1.3 collective-permute-done.1
  247.4 9.0 %all_to_all.50 = bf16[2,1024,128]{1,2,0:T(8,128)(2,1)S(1)} all-to-all(bf16[2,1024,128]{1,2,0:T(8,128)(2,1)S(1)} %bitcast.137), channel_id=1, replica_groups=mesh['sec'=4,'row'=4,'col'=2] {'col'}, dimensions={0} | all-to-all | bytes 1048576 | tf_op jit(solution)/shard_map/all_to_all | solution.py:9
  257.3 16.3 %fusion.22 = f32[2,4096,128]{1,2,0:T(8,128)S(1)} fusion(bf16[2048,128,1]{0,1,2:T(8,128)(2,1)S(1)} %reshape.101, bf16[1,2,4096,2048]{3,2,1,0:T(8,128)(2,1)} %param.5), kind=kOutput, calls=%fused_computation.18 | convolution fusion | flops 4294967296 | bytes 38273024 | tf_op jit(solution)/shard_map/kij,jb->kib/dot_general | solution.py:35
  275.0 32.0 %reduce-scatter.17.cloned.1.call-done = bf16[1024,128]{0,1:T(8,128)(2,1)} async-done(((bf16[4096,128]{0,1:T(8,128)(2,1)}), bf16[1024,128]{0,1:T(8,128)(2,1)}) %reduce-scatter.17.cloned.1.call-update) | async-done | bytes 262160 | tf_op jit(solution)/shard_map/reduce_scatter | solution.py:39
  309.1 26.5 %all-gather.9.cloned.1.call-done = bf16[4096,128]{0,1:T(8,128)(2,1)} async-done(((bf16[1024,128]{0,1:T(8,128)(2,1)}), bf16[4096,128]{0,1:T(8,128)(2,1)}) %all-gather.9.cloned.1.call-update) | async-done | bytes 1048592 | tf_op jit(solution)/shard_map/all_gather | solution.py:48
  335.6 13.2 %fusion.34 = f32[2,2048,128]{1,2,0:T(8,128)S(1)} fusion(bf16[1,2,4096,2048]{3,2,1,0:T(8,128)(2,1)} %param.5, bf16[4096,128]{0,1:T(8,128)(2,1)} %all-gather.9.cloned.1.call-done), kind=kOutput, calls=%fused_computation.22 | convolution fusion | flops 4294967296 | bytes 36700160 | tf_op jit(solution)/shard_map/kij,ib->kjb/dot_general | solution.py:45
  349.9 14.2 %reduce-scatter.19.cloned.1.call-done = bf16[1024,128]{0,1:T(8,128)(2,1)} async-done(((bf16[2048,128]{0,1:T(8,128)(2,1)}), bf16[1024,128]{0,1:T(8,128)(2,1)}) %reduce-scatter.19.cloned.1.call-update) | async-done | bytes 262160 | tf_op jit(solution)/shard_map/reduce_scatter | solution.py:52
  364.0 1.7 collective-permute-start.2
  365.8 1.3 collective-permute-done.2
  367.4 9.0 %all_to_all.51 = bf16[2,1024,128]{1,2,0:T(8,128)(2,1)S(1)} all-to-all(bf16[2,1024,128]{1,2,0:T(8,128)(2,1)S(1)} %bitcast.139), channel_id=1, replica_groups=mesh['sec'=4,'row'=4,'col'=2] {'col'}, dimensions={0} | all-to-all | bytes 1048576 | tf_op jit(solution)/shard_map/all_to_all | solution.py:9
  377.3 16.3 %fusion.25 = f32[2,4096,128]{1,2,0:T(8,128)S(1)} fusion(bf16[2048,128,1]{0,1,2:T(8,128)(2,1)S(1)} %reshape.103, bf16[1,2,4096,2048]{3,2,1,0:T(8,128)(2,1)} %param.5), kind=kOutput, calls=%fused_computation.19 | convolution fusion | flops 4294967296 | bytes 38273024 | tf_op jit(solution)/shard_map/kij,jb->kib/dot_general | solution.py:35
  395.0 32.0 %reduce-scatter.21.cloned.1.call-done = bf16[1024,128]{0,1:T(8,128)(2,1)} async-done(((bf16[4096,128]{0,1:T(8,128)(2,1)}), bf16[1024,128]{0,1:T(8,128)(2,1)}) %reduce-scatter.21.cloned.1.call-update) | async-done | bytes 262160 | tf_op jit(solution)/shard_map/reduce_scatter | solution.py:39
  428.9 26.7 %all-gather.11.cloned.1.call-done = bf16[4096,128]{0,1:T(8,128)(2,1)} async-done(((bf16[1024,128]{0,1:T(8,128)(2,1)}), bf16[4096,128]{0,1:T(8,128)(2,1)}) %all-gather.11.cloned.1.call-update) | async-done | bytes 1048592 | tf_op jit(solution)/shard_map/all_gather | solution.py:48
  455.6 13.2 %fusion.37 = f32[2,2048,128]{1,2,0:T(8,128)S(1)} fusion(bf16[1,2,4096,2048]{3,2,1,0:T(8,128)(2,1)} %param.5, bf16[4096,128]{0,1:T(8,128)(2,1)} %all-gather.11.cloned.1.call-done), kind=kOutput, calls=%fused_computation.23 | convolution fusion | flops 4294967296 | bytes 36700160 | tf_op jit(solution)/shard_map/kij,ib->kjb/dot_general | solution.py:45
  469.8 14.2 %reduce-scatter.23.cloned.1.call-done = bf16[1024,128]{0,1:T(8,128)(2,1)} async-done(((bf16[2048,128]{0,1:T(8,128)(2,1)}), bf16[1024,128]{0,1:T(8,128)(2,1)}) %reduce-scatter.23.cloned.1.call-update) | async-done | bytes 262160 | tf_op jit(solution)/shard_map/reduce_scatter | solution.py:52
  484.0 1.1 select_bitcast_fusion
  (90 shorter events, 24.1 us)
Async XLA Ops:
  6.5 60.6 %reduce-scatter.9.cloned.1.call-start = ((), (), s32[]{:S(2)}) async-start(), calls=%async_computation.12 | async-start | bytes 1310720 | tf_op jit(solution)/shard_map/reduce_scatter | solution.py:39
  39.4 56.3 %all-gather.5.cloned.1.call-start = ((), (), s32[]{:S(2)}) async-start(), calls=%async_computation.13 | async-start | bytes 1310720 | tf_op jit(solution)/shard_map/all_gather | solution.py:48
  68.9 55.1 %reduce-scatter.11.cloned.1.call-start = ((), (), s32[]{:S(2)}) async-start(), calls=%async_computation.14 | async-start | bytes 786432 | tf_op jit(solution)/shard_map/reduce_scatter | solution.py:52
  109.9 77.2 %reduce-scatter.13.cloned.1.call-start = ((), (), s32[]{:S(2)}) async-start(), calls=%async_computation.15 | async-start | bytes 1310720 | tf_op jit(solution)/shard_map/reduce_scatter | solution.py:39
  124.1 3.1 collective-permute-start
  155.0 60.7 %all-gather.7.cloned.1.call-start = ((), (), s32[]{:S(2)}) async-start(), calls=%async_computation.16 | async-start | bytes 1310720 | tf_op jit(solution)/shard_map/all_gather | solution.py:48
  188.9 55.1 %reduce-scatter.15.cloned.1.call-start = ((), (), s32[]{:S(2)}) async-start(), calls=%async_computation.17 | async-start | bytes 786432 | tf_op jit(solution)/shard_map/reduce_scatter | solution.py:52
  229.8 77.2 %reduce-scatter.17.cloned.1.call-start = ((), (), s32[]{:S(2)}) async-start(), calls=%async_computation.18 | async-start | bytes 1310720 | tf_op jit(solution)/shard_map/reduce_scatter | solution.py:39
  244.0 3.1 collective-permute-start.1
  275.0 60.7 %all-gather.9.cloned.1.call-start = ((), (), s32[]{:S(2)}) async-start(), calls=%async_computation.19 | async-start | bytes 1310720 | tf_op jit(solution)/shard_map/all_gather | solution.py:48
  308.9 55.1 %reduce-scatter.19.cloned.1.call-start = ((), (), s32[]{:S(2)}) async-start(), calls=%async_computation.20 | async-start | bytes 786432 | tf_op jit(solution)/shard_map/reduce_scatter | solution.py:52
  349.8 77.2 %reduce-scatter.21.cloned.1.call-start = ((), (), s32[]{:S(2)}) async-start(), calls=%async_computation.21 | async-start | bytes 1310720 | tf_op jit(solution)/shard_map/reduce_scatter | solution.py:39
  364.0 3.1 collective-permute-start.2
  394.9 60.7 %all-gather.11.cloned.1.call-start = ((), (), s32[]{:S(2)}) async-start(), calls=%async_computation.22 | async-start | bytes 1310720 | tf_op jit(solution)/shard_map/all_gather | solution.py:48
  428.8 55.2 %reduce-scatter.23.cloned.1.call-start = ((), (), s32[]{:S(2)}) async-start(), calls=%async_computation.23 | async-start | bytes 786432 | tf_op jit(solution)/shard_map/reduce_scatter | solution.py:52
  468.8 15.2 %copy-start = (bf16[1024,128]{0,1:T(8,128)(2,1)S(1)}, bf16[1024,128]{0,1:T(8,128)(2,1)}, u32[]{:S(2)}) copy-start(bf16[1024,128]{0,1:T(8,128)(2,1)} %reduce-scatter.11.cloned.1.call-done) | copy-start | bytes 786436
  468.8 15.2 %copy-start.1 = (bf16[1024,128]{0,1:T(8,128)(2,1)S(1)}, bf16[1024,128]{0,1:T(8,128)(2,1)}, u32[]{:S(2)}) copy-start(bf16[1024,128]{0,1:T(8,128)(2,1)} %reduce-scatter.15.cloned.1.call-done) | copy-start | bytes 786436
  468.8 15.2 %copy-start.2 = (bf16[1024,128]{0,1:T(8,128)(2,1)S(1)}, bf16[1024,128]{0,1:T(8,128)(2,1)}, u32[]{:S(2)}) copy-start(bf16[1024,128]{0,1:T(8,128)(2,1)} %reduce-scatter.19.cloned.1.call-done) | copy-start | bytes 786436
Sparse Core Ops, SparseCore 0:
  39.5 27.5 reduce-scatter.8
  69.1 26.5 all-gather.4
  110.0 14.0 reduce-scatter.10
  155.1 31.9 reduce-scatter.12
  189.0 26.5 all-gather.6
  229.9 14.0 reduce-scatter.14
  275.1 31.9 reduce-scatter.16
  309.0 26.5 all-gather.8
  349.9 14.0 reduce-scatter.18
  395.1 31.9 reduce-scatter.20
  429.0 26.5 all-gather.10
  469.9 14.0 reduce-scatter.22
